TPU v7x, 32 devices: a whole 2x2x4 slice. The times are simulated.
32 devices in a mesh: blk: 16 (over z, x, core), narrow: 2 (over y).
Axes of the slice: x: 2, y: 2, z: 4, core: 2. Of those that a mesh axis runs over, the one named last changes fastest.
Arguments:
- rhs: float32 [6144, 256], P('blk', 'narrow'), may hold values from -6 to 6
- zo: float32 [6144, 64], P('blk'), may hold values from -0.109375 to 0.109375
- e_diag: float32 [64, 96, 96], P('blk'), may hold values from -0.18 to 0.18
- a_off: float32 [64, 3, 96, 96], P('blk'), may hold values from -0.18 to 0.18
- e_off: float32 [64, 3, 96, 96], P('blk'), may hold values from -0.09 to 0.09
- col_index: int32 [64, 3], P('blk'), may hold values from 0 to 63, as said below
- inv_diag: float32 [2, 64, 96, 96], P(None, 'blk'), may hold values from -0.625 to 0.625
- shifts: float32 [2], replicated, may hold values from 0.5 to 2
Outputs:
- residual: float32 [6144, 256], P('blk', 'narrow')
- cross: float32 [64, 2, 256], P(('blk', 'narrow'))
Inputs may be any that keep to these rules, and one draw needn't show every extreme that they name: `col_index`: each block column index differs from its own block row by 1 or 2 in either direction, near the ends of the range reflected to the other side; the three indices of a row may repeat.
All inputs are finite; a program needn't handle non-finite values.
Results may differ from a plain program's by a relative error of at most 0.0001.
Values sent between devices are 32-bit elements; how exact they have to be, the bound alone decides.
A program may use at most 64 MiB of HBM per device.

v0:
```python
import jax
import jax.numpy as jnp
from jax import lax
from jax.sharding import PartitionSpec as P

SWEEPS = 8
precise = lax.Precision.HIGHEST


def extended_2(cells, sides, width):
    for axis, dim in sides:
        count = lax.axis_size(axis)
        ends = count - 1
        head = lax.slice_in_dim(cells, 0, width, axis=dim)
        tail = lax.slice_in_dim(cells, cells.shape[dim] - width, cells.shape[dim], axis=dim)
        cells = jnp.concatenate(
            [
                lax.ppermute(tail, axis, [(i, (i + 1) % count) for i in range(ends)]),
                cells,
                lax.ppermute(head, axis, [((i + 1) % count, i) for i in range(ends)]),
            ],
            axis=dim,
        )
    return cells


def block_product(matrices, field):
    return jnp.einsum("nab,nbk->nak", matrices, field, precision=precise)


def shards(rhs, zo, e_diag, a_off, e_off, col_index, inv_diag, shifts):
    row_count, col_width = rhs.shape
    blocks = e_diag.shape[0]
    block_size = e_diag.shape[1]
    local_col = col_index - lax.axis_index("blk") * blocks + 2

    def coupled(coupling, field):
        padded = extended_2(field.reshape(row_count, col_width), (("blk", 0),), 2 * block_size)
        extended = padded.reshape(blocks + 4, block_size, col_width)
        picked = jnp.take(extended, local_col, axis=0)
        return jnp.einsum("nsab,nsbk->nak", coupling, picked, precision=precise)

    current = rhs.reshape(blocks, block_size, col_width)
    images = []
    for which in range(2):
        shift_value = shifts[which]
        coupling = a_off - shift_value * e_off
        inverse = inv_diag[which]
        iterate = block_product(inverse, current)
        for sweep in range(SWEEPS):
            iterate = block_product(inverse, current - coupled(coupling, iterate))
        mass_image = block_product(e_diag, iterate) + coupled(e_off, iterate)
        current = current + 2.0 * shift_value * mass_image
        images.append(jnp.sqrt(2.0 * shift_value) * mass_image)
    stacked = jnp.stack(images, axis=2).reshape(row_count, 2, col_width)
    summed = lax.psum_scatter(
        jnp.einsum("ro,rsk->osk", zo, stacked, precision=precise),
        "blk",
        scatter_dimension=0,
        tiled=True,
    )
    cross = lax.all_to_all(summed, "narrow", split_axis=0, concat_axis=2, tiled=True)
    return (current.reshape(row_count, col_width), cross)


def solution(mesh):
    placed = (
        P("blk", "narrow"),
        P("blk", None),
        P("blk", None, None),
        P("blk", None, None, None),
        P("blk", None, None, None),
        P("blk", None),
        P(None, "blk", None, None),
        P(),
    )
    return jax.shard_map(
        shards,
        mesh=mesh,
        in_specs=placed,
        out_specs=(P("blk", "narrow"), P(("blk", "narrow"), None, None)),
        check_vma=False,
    )
```

profile of v0, /device:TPU:8, one launch (start us, length us, event | category | flops | bytes accessed | tf_op | source)
XLA Modules:
  0.0 328.5 jit_solution(1364033609867359985)
XLA Ops:
  7.2 1.4 fusion.107
  8.7 1.9 collective-permute-start
  10.6 4.5 %collective-permute-start.1 = (f32[192,128]{1,0:T(8,128)S(1)}, f32[192,128]{1,0:T(8,128)S(1)}, u32[]{:S(2)}, u32[]{:S(2)}) collective-permute-start(f32[192,128]{1,0:T(8,128)S(1)} %bitcast.399), channel_id=1, source_target_pairs={{2,0},{4,2},{6,4},{8,6},{10,8},{12,10},{14,12},{16,14},{18,16},{20... | collective-permute-start | bytes 294920 | tf_op jit(solution)/shard_map/ppermute | solution.py:20
  17.1 2.5 multiply_subtract_fusion
  22.1 1.3 fusion.105
  23.3 1.9 collective-permute-start.2
  25.3 4.5 %collective-permute-start.3 = (f32[192,128]{1,0:T(8,128)S(1)}, f32[192,128]{1,0:T(8,128)S(1)}, u32[]{:S(2)}, u32[]{:S(2)}) collective-permute-start(f32[192,128]{1,0:T(8,128)S(1)} %bitcast.406), channel_id=1, source_target_pairs={{2,0},{4,2},{6,4},{8,6},{10,8},{12,10},{14,12},{16,14},{18,16},{20... | collective-permute-start | bytes 294920 | tf_op jit(solution)/shard_map/ppermute | solution.py:20
  30.2 1.8 collective-permute-done.3
  35.0 1.9 collective-permute-start.4
  36.9 4.6 %collective-permute-start.5 = (f32[192,128]{1,0:T(8,128)S(1)}, f32[192,128]{1,0:T(8,128)S(1)}, u32[]{:S(2)}, u32[]{:S(2)}) collective-permute-start(f32[192,128]{1,0:T(8,128)S(1)} %bitcast.407), channel_id=1, source_target_pairs={{2,0},{4,2},{6,4},{8,6},{10,8},{12,10},{14,12},{16,14},{18,16},{20... | collective-permute-start | bytes 294920 | tf_op jit(solution)/shard_map/ppermute | solution.py:20
  41.9 1.8 collective-permute-done.5
  45.4 1.3 fusion.101
  46.7 2.6 collective-permute-start.6
  49.3 3.9 %collective-permute-start.7 = (f32[192,128]{1,0:T(8,128)S(1)}, f32[192,128]{1,0:T(8,128)S(1)}, u32[]{:S(2)}, u32[]{:S(2)}) collective-permute-start(f32[192,128]{1,0:T(8,128)S(1)} %bitcast.408), channel_id=1, source_target_pairs={{2,0},{4,2},{6,4},{8,6},{10,8},{12,10},{14,12},{16,14},{18,16},{20... | collective-permute-start | bytes 294920 | tf_op jit(solution)/shard_map/ppermute | solution.py:20
  53.6 1.8 collective-permute-done.7
  57.2 1.3 fusion.99
  58.4 2.6 collective-permute-start.8
  61.0 4.0 %collective-permute-start.9 = (f32[192,128]{1,0:T(8,128)S(1)}, f32[192,128]{1,0:T(8,128)S(1)}, u32[]{:S(2)}, u32[]{:S(2)}) collective-permute-start(f32[192,128]{1,0:T(8,128)S(1)} %bitcast.409), channel_id=1, source_target_pairs={{2,0},{4,2},{6,4},{8,6},{10,8},{12,10},{14,12},{16,14},{18,16},{20... | collective-permute-start | bytes 294920 | tf_op jit(solution)/shard_map/ppermute | solution.py:20
  65.4 1.8 collective-permute-done.9
  68.9 1.3 fusion.97
  70.2 2.6 collective-permute-start.10
  72.8 3.9 %collective-permute-start.11 = (f32[192,128]{1,0:T(8,128)S(1)}, f32[192,128]{1,0:T(8,128)S(1)}, u32[]{:S(2)}, u32[]{:S(2)}) collective-permute-start(f32[192,128]{1,0:T(8,128)S(1)} %bitcast.410), channel_id=1, source_target_pairs={{2,0},{4,2},{6,4},{8,6},{10,8},{12,10},{14,12},{16,14},{18,16},{20... | collective-permute-start | bytes 294920 | tf_op jit(solution)/shard_map/ppermute | solution.py:20
  77.1 1.8 collective-permute-done.11
  80.6 1.3 fusion.95
  81.9 2.6 collective-permute-start.12
  84.5 4.0 %collective-permute-start.13 = (f32[192,128]{1,0:T(8,128)S(1)}, f32[192,128]{1,0:T(8,128)S(1)}, u32[]{:S(2)}, u32[]{:S(2)}) collective-permute-start(f32[192,128]{1,0:T(8,128)S(1)} %bitcast.411), channel_id=1, source_target_pairs={{2,0},{4,2},{6,4},{8,6},{10,8},{12,10},{14,12},{16,14},{18,16},{20... | collective-permute-start | bytes 294920 | tf_op jit(solution)/shard_map/ppermute | solution.py:20
  88.8 1.8 collective-permute-done.13
  92.3 1.3 fusion.93
  93.6 2.6 collective-permute-start.14
  96.2 4.1 %collective-permute-start.15 = (f32[192,128]{1,0:T(8,128)S(1)}, f32[192,128]{1,0:T(8,128)S(1)}, u32[]{:S(2)}, u32[]{:S(2)}) collective-permute-start(f32[192,128]{1,0:T(8,128)S(1)} %bitcast.412), channel_id=1, source_target_pairs={{2,0},{4,2},{6,4},{8,6},{10,8},{12,10},{14,12},{16,14},{18,16},{20... | collective-permute-start | bytes 294920 | tf_op jit(solution)/shard_map/ppermute | solution.py:20
  100.6 1.8 collective-permute-done.15
  105.4 2.6 collective-permute-start.16
  108.0 3.9 %collective-permute-start.17 = (f32[192,128]{1,0:T(8,128)S(1)}, f32[192,128]{1,0:T(8,128)S(1)}, u32[]{:S(2)}, u32[]{:S(2)}) collective-permute-start(f32[192,128]{1,0:T(8,128)S(1)} %bitcast.404), channel_id=1, source_target_pairs={{2,0},{4,2},{6,4},{8,6},{10,8},{12,10},{14,12},{16,14},{18,16},{20... | collective-permute-start | bytes 294920 | tf_op jit(solution)/shard_map/ppermute | solution.py:20
  112.6 1.6 collective-permute-done.17
  117.7 2.6 collective-permute-start.18
  120.3 3.9 %collective-permute-start.19 = (f32[192,128]{1,0:T(8,128)S(1)}, f32[192,128]{1,0:T(8,128)S(1)}, u32[]{:S(2)}, u32[]{:S(2)}) collective-permute-start(f32[192,128]{1,0:T(8,128)S(1)} %bitcast.413), channel_id=1, source_target_pairs={{2,0},{4,2},{6,4},{8,6},{10,8},{12,10},{14,12},{16,14},{18,16},{20... | collective-permute-start | bytes 294920 | tf_op jit(solution)/shard_map/ppermute | solution.py:20
  124.7 1.8 collective-permute-done.19
  128.1 1.3 fusion.87
  129.3 2.6 collective-permute-start.20
  132.0 3.9 %collective-permute-start.21 = (f32[192,128]{1,0:T(8,128)S(1)}, f32[192,128]{1,0:T(8,128)S(1)}, u32[]{:S(2)}, u32[]{:S(2)}) collective-permute-start(f32[192,128]{1,0:T(8,128)S(1)} %bitcast.414), channel_id=1, source_target_pairs={{2,0},{4,2},{6,4},{8,6},{10,8},{12,10},{14,12},{16,14},{18,16},{20... | collective-permute-start | bytes 294920 | tf_op jit(solution)/shard_map/ppermute | solution.py:20
  136.3 1.8 collective-permute-done.21
  141.1 2.6 collective-permute-start.22
  143.7 3.9 %collective-permute-start.23 = (f32[192,128]{1,0:T(8,128)S(1)}, f32[192,128]{1,0:T(8,128)S(1)}, u32[]{:S(2)}, u32[]{:S(2)}) collective-permute-start(f32[192,128]{1,0:T(8,128)S(1)} %bitcast.415), channel_id=1, source_target_pairs={{2,0},{4,2},{6,4},{8,6},{10,8},{12,10},{14,12},{16,14},{18,16},{20... | collective-permute-start | bytes 294920 | tf_op jit(solution)/shard_map/ppermute | solution.py:20
  148.0 1.8 collective-permute-done.23
  152.8 2.6 collective-permute-start.24
  155.4 3.9 %collective-permute-start.25 = (f32[192,128]{1,0:T(8,128)S(1)}, f32[192,128]{1,0:T(8,128)S(1)}, u32[]{:S(2)}, u32[]{:S(2)}) collective-permute-start(f32[192,128]{1,0:T(8,128)S(1)} %bitcast.416), channel_id=1, source_target_pairs={{2,0},{4,2},{6,4},{8,6},{10,8},{12,10},{14,12},{16,14},{18,16},{20... | collective-permute-start | bytes 294920 | tf_op jit(solution)/shard_map/ppermute | solution.py:20
  159.7 1.8 collective-permute-done.25
  164.5 2.6 collective-permute-start.26
  167.2 3.9 %collective-permute-start.27 = (f32[192,128]{1,0:T(8,128)S(1)}, f32[192,128]{1,0:T(8,128)S(1)}, u32[]{:S(2)}, u32[]{:S(2)}) collective-permute-start(f32[192,128]{1,0:T(8,128)S(1)} %bitcast.417), channel_id=1, source_target_pairs={{2,0},{4,2},{6,4},{8,6},{10,8},{12,10},{14,12},{16,14},{18,16},{20... | collective-permute-start | bytes 294920 | tf_op jit(solution)/shard_map/ppermute | solution.py:20
  171.5 1.8 collective-permute-done.27
  176.3 2.6 collective-permute-start.28
  178.9 3.9 %collective-permute-start.29 = (f32[192,128]{1,0:T(8,128)S(1)}, f32[192,128]{1,0:T(8,128)S(1)}, u32[]{:S(2)}, u32[]{:S(2)}) collective-permute-start(f32[192,128]{1,0:T(8,128)S(1)} %bitcast.418), channel_id=1, source_target_pairs={{2,0},{4,2},{6,4},{8,6},{10,8},{12,10},{14,12},{16,14},{18,16},{20... | collective-permute-start | bytes 294920 | tf_op jit(solution)/shard_map/ppermute | solution.py:20
  183.2 1.8 collective-permute-done.29
  188.0 2.6 collective-permute-start.30
  190.6 4.2 %collective-permute-start.31 = (f32[192,128]{1,0:T(8,128)S(1)}, f32[192,128]{1,0:T(8,128)S(1)}, u32[]{:S(2)}, u32[]{:S(2)}) collective-permute-start(f32[192,128]{1,0:T(8,128)S(1)} %bitcast.419), channel_id=1, source_target_pairs={{2,0},{4,2},{6,4},{8,6},{10,8},{12,10},{14,12},{16,14},{18,16},{20... | collective-permute-start | bytes 294920 | tf_op jit(solution)/shard_map/ppermute | solution.py:20
  194.9 1.8 collective-permute-done.31
  199.7 2.6 collective-permute-start.32
  202.3 3.9 %collective-permute-start.33 = (f32[192,128]{1,0:T(8,128)S(1)}, f32[192,128]{1,0:T(8,128)S(1)}, u32[]{:S(2)}, u32[]{:S(2)}) collective-permute-start(f32[192,128]{1,0:T(8,128)S(1)} %bitcast.401), channel_id=1, source_target_pairs={{2,0},{4,2},{6,4},{8,6},{10,8},{12,10},{14,12},{16,14},{18,16},{20... | collective-permute-start | bytes 294920 | tf_op jit(solution)/shard_map/ppermute | solution.py:20
  207.0 1.4 collective-permute-done.33
  210.4 2.6 collective-permute-start.34
  213.0 3.9 %collective-permute-start.35 = (f32[192,128]{1,0:T(8,128)S(1)}, f32[192,128]{1,0:T(8,128)S(1)}, u32[]{:S(2)}, u32[]{:S(2)}) collective-permute-start(f32[192,128]{1,0:T(8,128)S(1)} %bitcast.402), channel_id=1, source_target_pairs={{2,0},{4,2},{6,4},{8,6},{10,8},{12,10},{14,12},{16,14},{18,16},{20... | collective-permute-start | bytes 294920 | tf_op jit(solution)/shard_map/ppermute | solution.py:20
  217.3 1.8 collective-permute-done.35
  225.6 88.5 %all-reduce.3.cloned.1.call-done = f32[64,2,128]{2,0,1:T(8,128)} async-done(((f32[64,2,128]{2,0,1:T(8,128)}), f32[64,2,128]{2,0,1:T(8,128)}) %all-reduce.3.cloned.1.call-update) | async-done | bytes 65552
  314.7 6.3 %all_to_all.18 = f32[4,2,128]{2,1,0:T(2,128)S(1)} all-to-all(f32[4,2,128]{2,1,0:T(2,128)S(1)} %copy.11), channel_id=1, replica_groups=mesh['blk'=16,'narrow'=2] {'narrow'}, dimensions={0} | all-to-all | bytes 8192 | tf_op jit(solution)/shard_map/all_to_all | solution.py:62
  (136 shorter events, 55.2 us)
Async XLA Ops:
  7.2 109.2 %copy-start = (f32[4,96,96]{2,1,0:T(8,128)S(1)}, f32[4,96,96]{2,1,0:T(8,128)}, u32[]{:S(2)}) copy-start(f32[4,96,96]{2,1,0:T(8,128)} %param.12) | copy-start | bytes 442372
  7.2 9.9 %copy-start.3 = (f32[4,3,96,96]{3,2,1,0:T(8,128)S(1)}, f32[4,3,96,96]{3,2,1,0:T(8,128)}, u32[]{:S(2)}) copy-start(f32[4,3,96,96]{3,2,1,0:T(8,128)} %param.14) | copy-start | bytes 1327108
  7.2 306.8 %all-reduce.3.cloned.1.call-start = ((), (), s32[]{:S(2)}) async-start(), calls=%async_computation.1 | async-start | bytes 131072
  8.7 10.9 %collective-permute-start = (f32[192,128]{1,0:T(8,128)S(1)}, f32[192,128]{1,0:T(8,128)S(1)}, u32[]{:S(2)}, u32[]{:S(2)}) collective-permute-start(f32[192,128]{1,0:T(8,128)S(1)} %bitcast.400), channel_id=1, source_target_pairs={{0,2},{2,4},{4,6},{6,8},{8,10},{10,12},{12,14},{14,16},{16,18},{18... | collective-permute-start | bytes 294920 | tf_op jit(solution)/shard_map/ppermute | solution.py:18
  10.6 9.0 %collective-permute-start.1 = (f32[192,128]{1,0:T(8,128)S(1)}, f32[192,128]{1,0:T(8,128)S(1)}, u32[]{:S(2)}, u32[]{:S(2)}) collective-permute-start(f32[192,128]{1,0:T(8,128)S(1)} %bitcast.399), channel_id=1, source_target_pairs={{2,0},{4,2},{6,4},{8,6},{10,8},{12,10},{14,12},{16,14},{18,16},{20... | collective-permute-start | bytes 294920 | tf_op jit(solution)/shard_map/ppermute | solution.py:20
  15.2 0.7 copy-start.7
  15.9 0.7 copy-start.8
  19.6 0.6 copy-start.4
  20.2 0.9 copy-start.2
  23.3 6.8 %collective-permute-start.2 = (f32[192,128]{1,0:T(8,128)S(1)}, f32[192,128]{1,0:T(8,128)S(1)}, u32[]{:S(2)}, u32[]{:S(2)}) collective-permute-start(f32[192,128]{1,0:T(8,128)S(1)} %bitcast.421), channel_id=1, source_target_pairs={{0,2},{2,4},{4,6},{6,8},{8,10},{10,12},{12,14},{14,16},{16,18},{18... | collective-permute-start | bytes 294920 | tf_op jit(solution)/shard_map/ppermute | solution.py:18
  25.3 6.7 %collective-permute-start.3 = (f32[192,128]{1,0:T(8,128)S(1)}, f32[192,128]{1,0:T(8,128)S(1)}, u32[]{:S(2)}, u32[]{:S(2)}) collective-permute-start(f32[192,128]{1,0:T(8,128)S(1)} %bitcast.406), channel_id=1, source_target_pairs={{2,0},{4,2},{6,4},{8,6},{10,8},{12,10},{14,12},{16,14},{18,16},{20... | collective-permute-start | bytes 294920 | tf_op jit(solution)/shard_map/ppermute | solution.py:20
  35.0 6.9 %collective-permute-start.4 = (f32[192,128]{1,0:T(8,128)S(1)}, f32[192,128]{1,0:T(8,128)S(1)}, u32[]{:S(2)}, u32[]{:S(2)}) collective-permute-start(f32[192,128]{1,0:T(8,128)S(1)} %bitcast.422), channel_id=1, source_target_pairs={{0,2},{2,4},{4,6},{6,8},{8,10},{10,12},{12,14},{14,16},{16,18},{18... | collective-permute-start | bytes 294920 | tf_op jit(solution)/shard_map/ppermute | solution.py:18
  36.9 6.8 %collective-permute-start.5 = (f32[192,128]{1,0:T(8,128)S(1)}, f32[192,128]{1,0:T(8,128)S(1)}, u32[]{:S(2)}, u32[]{:S(2)}) collective-permute-start(f32[192,128]{1,0:T(8,128)S(1)} %bitcast.407), channel_id=1, source_target_pairs={{2,0},{4,2},{6,4},{8,6},{10,8},{12,10},{14,12},{16,14},{18,16},{20... | collective-permute-start | bytes 294920 | tf_op jit(solution)/shard_map/ppermute | solution.py:20
  46.7 6.9 %collective-permute-start.6 = (f32[192,128]{1,0:T(8,128)S(1)}, f32[192,128]{1,0:T(8,128)S(1)}, u32[]{:S(2)}, u32[]{:S(2)}) collective-permute-start(f32[192,128]{1,0:T(8,128)S(1)} %bitcast.423), channel_id=1, source_target_pairs={{0,2},{2,4},{4,6},{6,8},{8,10},{10,12},{12,14},{14,16},{16,18},{18... | collective-permute-start | bytes 294920 | tf_op jit(solution)/shard_map/ppermute | solution.py:18
  49.3 6.1 %collective-permute-start.7 = (f32[192,128]{1,0:T(8,128)S(1)}, f32[192,128]{1,0:T(8,128)S(1)}, u32[]{:S(2)}, u32[]{:S(2)}) collective-permute-start(f32[192,128]{1,0:T(8,128)S(1)} %bitcast.408), channel_id=1, source_target_pairs={{2,0},{4,2},{6,4},{8,6},{10,8},{12,10},{14,12},{16,14},{18,16},{20... | collective-permute-start | bytes 294920 | tf_op jit(solution)/shard_map/ppermute | solution.py:20
  58.4 6.9 %collective-permute-start.8 = (f32[192,128]{1,0:T(8,128)S(1)}, f32[192,128]{1,0:T(8,128)S(1)}, u32[]{:S(2)}, u32[]{:S(2)}) collective-permute-start(f32[192,128]{1,0:T(8,128)S(1)} %bitcast.424), channel_id=1, source_target_pairs={{0,2},{2,4},{4,6},{6,8},{8,10},{10,12},{12,14},{14,16},{16,18},{18... | collective-permute-start | bytes 294920 | tf_op jit(solution)/shard_map/ppermute | solution.py:18
  61.0 6.2 %collective-permute-start.9 = (f32[192,128]{1,0:T(8,128)S(1)}, f32[192,128]{1,0:T(8,128)S(1)}, u32[]{:S(2)}, u32[]{:S(2)}) collective-permute-start(f32[192,128]{1,0:T(8,128)S(1)} %bitcast.409), channel_id=1, source_target_pairs={{2,0},{4,2},{6,4},{8,6},{10,8},{12,10},{14,12},{16,14},{18,16},{20... | collective-permute-start | bytes 294920 | tf_op jit(solution)/shard_map/ppermute | solution.py:20
  70.2 6.9 %collective-permute-start.10 = (f32[192,128]{1,0:T(8,128)S(1)}, f32[192,128]{1,0:T(8,128)S(1)}, u32[]{:S(2)}, u32[]{:S(2)}) collective-permute-start(f32[192,128]{1,0:T(8,128)S(1)} %bitcast.425), channel_id=1, source_target_pairs={{0,2},{2,4},{4,6},{6,8},{8,10},{10,12},{12,14},{14,16},{16,18},{18... | collective-permute-start | bytes 294920 | tf_op jit(solution)/shard_map/ppermute | solution.py:18
  72.8 6.1 %collective-permute-start.11 = (f32[192,128]{1,0:T(8,128)S(1)}, f32[192,128]{1,0:T(8,128)S(1)}, u32[]{:S(2)}, u32[]{:S(2)}) collective-permute-start(f32[192,128]{1,0:T(8,128)S(1)} %bitcast.410), channel_id=1, source_target_pairs={{2,0},{4,2},{6,4},{8,6},{10,8},{12,10},{14,12},{16,14},{18,16},{20... | collective-permute-start | bytes 294920 | tf_op jit(solution)/shard_map/ppermute | solution.py:20
  81.9 6.9 %collective-permute-start.12 = (f32[192,128]{1,0:T(8,128)S(1)}, f32[192,128]{1,0:T(8,128)S(1)}, u32[]{:S(2)}, u32[]{:S(2)}) collective-permute-start(f32[192,128]{1,0:T(8,128)S(1)} %bitcast.426), channel_id=1, source_target_pairs={{0,2},{2,4},{4,6},{6,8},{8,10},{10,12},{12,14},{14,16},{16,18},{18... | collective-permute-start | bytes 294920 | tf_op jit(solution)/shard_map/ppermute | solution.py:18
  84.5 6.2 %collective-permute-start.13 = (f32[192,128]{1,0:T(8,128)S(1)}, f32[192,128]{1,0:T(8,128)S(1)}, u32[]{:S(2)}, u32[]{:S(2)}) collective-permute-start(f32[192,128]{1,0:T(8,128)S(1)} %bitcast.411), channel_id=1, source_target_pairs={{2,0},{4,2},{6,4},{8,6},{10,8},{12,10},{14,12},{16,14},{18,16},{20... | collective-permute-start | bytes 294920 | tf_op jit(solution)/shard_map/ppermute | solution.py:20
  93.6 6.9 %collective-permute-start.14 = (f32[192,128]{1,0:T(8,128)S(1)}, f32[192,128]{1,0:T(8,128)S(1)}, u32[]{:S(2)}, u32[]{:S(2)}) collective-permute-start(f32[192,128]{1,0:T(8,128)S(1)} %bitcast.427), channel_id=1, source_target_pairs={{0,2},{2,4},{4,6},{6,8},{8,10},{10,12},{12,14},{14,16},{16,18},{18... | collective-permute-start | bytes 294920 | tf_op jit(solution)/shard_map/ppermute | solution.py:18
  96.2 6.1 %collective-permute-start.15 = (f32[192,128]{1,0:T(8,128)S(1)}, f32[192,128]{1,0:T(8,128)S(1)}, u32[]{:S(2)}, u32[]{:S(2)}) collective-permute-start(f32[192,128]{1,0:T(8,128)S(1)} %bitcast.412), channel_id=1, source_target_pairs={{2,0},{4,2},{6,4},{8,6},{10,8},{12,10},{14,12},{16,14},{18,16},{20... | collective-permute-start | bytes 294920 | tf_op jit(solution)/shard_map/ppermute | solution.py:20
  105.4 7.2 %collective-permute-start.16 = (f32[192,128]{1,0:T(8,128)S(1)}, f32[192,128]{1,0:T(8,128)S(1)}, u32[]{:S(2)}, u32[]{:S(2)}) collective-permute-start(f32[192,128]{1,0:T(8,128)S(1)} %bitcast.420), channel_id=1, source_target_pairs={{0,2},{2,4},{4,6},{6,8},{8,10},{10,12},{12,14},{14,16},{16,18},{18... | collective-permute-start | bytes 294920 | tf_op jit(solution)/shard_map/ppermute | solution.py:18
  108.0 6.1 %collective-permute-start.17 = (f32[192,128]{1,0:T(8,128)S(1)}, f32[192,128]{1,0:T(8,128)S(1)}, u32[]{:S(2)}, u32[]{:S(2)}) collective-permute-start(f32[192,128]{1,0:T(8,128)S(1)} %bitcast.404), channel_id=1, source_target_pairs={{2,0},{4,2},{6,4},{8,6},{10,8},{12,10},{14,12},{16,14},{18,16},{20... | collective-permute-start | bytes 294920 | tf_op jit(solution)/shard_map/ppermute | solution.py:20
  114.1 0.7 copy-start.5
  116.4 1.0 copy-start.1
  117.7 6.9 %collective-permute-start.18 = (f32[192,128]{1,0:T(8,128)S(1)}, f32[192,128]{1,0:T(8,128)S(1)}, u32[]{:S(2)}, u32[]{:S(2)}) collective-permute-start(f32[192,128]{1,0:T(8,128)S(1)} %bitcast.428), channel_id=1, source_target_pairs={{0,2},{2,4},{4,6},{6,8},{8,10},{10,12},{12,14},{14,16},{16,18},{18... | collective-permute-start | bytes 294920 | tf_op jit(solution)/shard_map/ppermute | solution.py:18
  120.3 6.1 %collective-permute-start.19 = (f32[192,128]{1,0:T(8,128)S(1)}, f32[192,128]{1,0:T(8,128)S(1)}, u32[]{:S(2)}, u32[]{:S(2)}) collective-permute-start(f32[192,128]{1,0:T(8,128)S(1)} %bitcast.413), channel_id=1, source_target_pairs={{2,0},{4,2},{6,4},{8,6},{10,8},{12,10},{14,12},{16,14},{18,16},{20... | collective-permute-start | bytes 294920 | tf_op jit(solution)/shard_map/ppermute | solution.py:20
  129.3 6.9 %collective-permute-start.20 = (f32[192,128]{1,0:T(8,128)S(1)}, f32[192,128]{1,0:T(8,128)S(1)}, u32[]{:S(2)}, u32[]{:S(2)}) collective-permute-start(f32[192,128]{1,0:T(8,128)S(1)} %bitcast.429), channel_id=1, source_target_pairs={{0,2},{2,4},{4,6},{6,8},{8,10},{10,12},{12,14},{14,16},{16,18},{18... | collective-permute-start | bytes 294920 | tf_op jit(solution)/shard_map/ppermute | solution.py:18
  132.0 6.1 %collective-permute-start.21 = (f32[192,128]{1,0:T(8,128)S(1)}, f32[192,128]{1,0:T(8,128)S(1)}, u32[]{:S(2)}, u32[]{:S(2)}) collective-permute-start(f32[192,128]{1,0:T(8,128)S(1)} %bitcast.414), channel_id=1, source_target_pairs={{2,0},{4,2},{6,4},{8,6},{10,8},{12,10},{14,12},{16,14},{18,16},{20... | collective-permute-start | bytes 294920 | tf_op jit(solution)/shard_map/ppermute | solution.py:20
  141.1 6.9 %collective-permute-start.22 = (f32[192,128]{1,0:T(8,128)S(1)}, f32[192,128]{1,0:T(8,128)S(1)}, u32[]{:S(2)}, u32[]{:S(2)}) collective-permute-start(f32[192,128]{1,0:T(8,128)S(1)} %bitcast.430), channel_id=1, source_target_pairs={{0,2},{2,4},{4,6},{6,8},{8,10},{10,12},{12,14},{14,16},{16,18},{18... | collective-permute-start | bytes 294920 | tf_op jit(solution)/shard_map/ppermute | solution.py:18
  143.7 6.1 %collective-permute-start.23 = (f32[192,128]{1,0:T(8,128)S(1)}, f32[192,128]{1,0:T(8,128)S(1)}, u32[]{:S(2)}, u32[]{:S(2)}) collective-permute-start(f32[192,128]{1,0:T(8,128)S(1)} %bitcast.415), channel_id=1, source_target_pairs={{2,0},{4,2},{6,4},{8,6},{10,8},{12,10},{14,12},{16,14},{18,16},{20... | collective-permute-start | bytes 294920 | tf_op jit(solution)/shard_map/ppermute | solution.py:20
  152.8 6.9 %collective-permute-start.24 = (f32[192,128]{1,0:T(8,128)S(1)}, f32[192,128]{1,0:T(8,128)S(1)}, u32[]{:S(2)}, u32[]{:S(2)}) collective-permute-start(f32[192,128]{1,0:T(8,128)S(1)} %bitcast.431), channel_id=1, source_target_pairs={{0,2},{2,4},{4,6},{6,8},{8,10},{10,12},{12,14},{14,16},{16,18},{18... | collective-permute-start | bytes 294920 | tf_op jit(solution)/shard_map/ppermute | solution.py:18
  155.4 6.1 %collective-permute-start.25 = (f32[192,128]{1,0:T(8,128)S(1)}, f32[192,128]{1,0:T(8,128)S(1)}, u32[]{:S(2)}, u32[]{:S(2)}) collective-permute-start(f32[192,128]{1,0:T(8,128)S(1)} %bitcast.416), channel_id=1, source_target_pairs={{2,0},{4,2},{6,4},{8,6},{10,8},{12,10},{14,12},{16,14},{18,16},{20... | collective-permute-start | bytes 294920 | tf_op jit(solution)/shard_map/ppermute | solution.py:20
  164.5 6.9 %collective-permute-start.26 = (f32[192,128]{1,0:T(8,128)S(1)}, f32[192,128]{1,0:T(8,128)S(1)}, u32[]{:S(2)}, u32[]{:S(2)}) collective-permute-start(f32[192,128]{1,0:T(8,128)S(1)} %bitcast.432), channel_id=1, source_target_pairs={{0,2},{2,4},{4,6},{6,8},{8,10},{10,12},{12,14},{14,16},{16,18},{18... | collective-permute-start | bytes 294920 | tf_op jit(solution)/shard_map/ppermute | solution.py:18
  167.2 6.1 %collective-permute-start.27 = (f32[192,128]{1,0:T(8,128)S(1)}, f32[192,128]{1,0:T(8,128)S(1)}, u32[]{:S(2)}, u32[]{:S(2)}) collective-permute-start(f32[192,128]{1,0:T(8,128)S(1)} %bitcast.417), channel_id=1, source_target_pairs={{2,0},{4,2},{6,4},{8,6},{10,8},{12,10},{14,12},{16,14},{18,16},{20... | collective-permute-start | bytes 294920 | tf_op jit(solution)/shard_map/ppermute | solution.py:20
  176.3 6.9 %collective-permute-start.28 = (f32[192,128]{1,0:T(8,128)S(1)}, f32[192,128]{1,0:T(8,128)S(1)}, u32[]{:S(2)}, u32[]{:S(2)}) collective-permute-start(f32[192,128]{1,0:T(8,128)S(1)} %bitcast.433), channel_id=1, source_target_pairs={{0,2},{2,4},{4,6},{6,8},{8,10},{10,12},{12,14},{14,16},{16,18},{18... | collective-permute-start | bytes 294920 | tf_op jit(solution)/shard_map/ppermute | solution.py:18
  178.9 6.1 %collective-permute-start.29 = (f32[192,128]{1,0:T(8,128)S(1)}, f32[192,128]{1,0:T(8,128)S(1)}, u32[]{:S(2)}, u32[]{:S(2)}) collective-permute-start(f32[192,128]{1,0:T(8,128)S(1)} %bitcast.418), channel_id=1, source_target_pairs={{2,0},{4,2},{6,4},{8,6},{10,8},{12,10},{14,12},{16,14},{18,16},{20... | collective-permute-start | bytes 294920 | tf_op jit(solution)/shard_map/ppermute | solution.py:20
  188.0 6.9 %collective-permute-start.30 = (f32[192,128]{1,0:T(8,128)S(1)}, f32[192,128]{1,0:T(8,128)S(1)}, u32[]{:S(2)}, u32[]{:S(2)}) collective-permute-start(f32[192,128]{1,0:T(8,128)S(1)} %bitcast.434), channel_id=1, source_target_pairs={{0,2},{2,4},{4,6},{6,8},{8,10},{10,12},{12,14},{14,16},{16,18},{18... | collective-permute-start | bytes 294920 | tf_op jit(solution)/shard_map/ppermute | solution.py:18
  190.6 6.1 %collective-permute-start.31 = (f32[192,128]{1,0:T(8,128)S(1)}, f32[192,128]{1,0:T(8,128)S(1)}, u32[]{:S(2)}, u32[]{:S(2)}) collective-permute-start(f32[192,128]{1,0:T(8,128)S(1)} %bitcast.419), channel_id=1, source_target_pairs={{2,0},{4,2},{6,4},{8,6},{10,8},{12,10},{14,12},{16,14},{18,16},{20... | collective-permute-start | bytes 294920 | tf_op jit(solution)/shard_map/ppermute | solution.py:20
  199.7 7.3 %collective-permute-start.32 = (f32[192,128]{1,0:T(8,128)S(1)}, f32[192,128]{1,0:T(8,128)S(1)}, u32[]{:S(2)}, u32[]{:S(2)}) collective-permute-start(f32[192,128]{1,0:T(8,128)S(1)} %bitcast.403), channel_id=1, source_target_pairs={{0,2},{2,4},{4,6},{6,8},{8,10},{10,12},{12,14},{14,16},{16,18},{18... | collective-permute-start | bytes 294920 | tf_op jit(solution)/shard_map/ppermute | solution.py:18
  202.3 6.1 %collective-permute-start.33 = (f32[192,128]{1,0:T(8,128)S(1)}, f32[192,128]{1,0:T(8,128)S(1)}, u32[]{:S(2)}, u32[]{:S(2)}) collective-permute-start(f32[192,128]{1,0:T(8,128)S(1)} %bitcast.401), channel_id=1, source_target_pairs={{2,0},{4,2},{6,4},{8,6},{10,8},{12,10},{14,12},{16,14},{18,16},{20... | collective-permute-start | bytes 294920 | tf_op jit(solution)/shard_map/ppermute | solution.py:20
  210.4 6.9 %collective-permute-start.34 = (f32[192,128]{1,0:T(8,128)S(1)}, f32[192,128]{1,0:T(8,128)S(1)}, u32[]{:S(2)}, u32[]{:S(2)}) collective-permute-start(f32[192,128]{1,0:T(8,128)S(1)} %bitcast.405), channel_id=1, source_target_pairs={{0,2},{2,4},{4,6},{6,8},{8,10},{10,12},{12,14},{14,16},{16,18},{18... | collective-permute-start | bytes 294920 | tf_op jit(solution)/shard_map/ppermute | solution.py:18
  213.0 6.1 %collective-permute-start.35 = (f32[192,128]{1,0:T(8,128)S(1)}, f32[192,128]{1,0:T(8,128)S(1)}, u32[]{:S(2)}, u32[]{:S(2)}) collective-permute-start(f32[192,128]{1,0:T(8,128)S(1)} %bitcast.402), channel_id=1, source_target_pairs={{2,0},{4,2},{6,4},{8,6},{10,8},{12,10},{14,12},{16,14},{18,16},{20... | collective-permute-start | bytes 294920 | tf_op jit(solution)/shard_map/ppermute | solution.py:20
  221.8 0.9 copy-start.6
  223.7 0.7 copy-start.9
Sparse Core Ops, SparseCore 0:
  223.8 90.1 all-reduce.2
where the time goes:
time: 330 us; the launch traced here: 329 us
  waiting for transfers between devices  124 us (38%)
  starting transfers between devices  118 us (36%)
  matrix products  39.9 us (12%)
  local copies, waits for them, and re-layouts  19.9 us (6%)
  between operations  17.1 us (5%)
  blocking collectives  6.32 us (2%)
    unnamed x2, waiting for transfers between devices  88.5 us
    ppermute x18, starting transfers between devices, extended_2(): lax.ppermute(head, axis, [((i + 1) % count, i) for i in range(ends)])  73.3 us
    ppermute x18, starting transfers between devices, extended_2(): lax.ppermute(tail, axis, [(i, (i + 1) % count) for i in range(ends)])  44.9 us
    ppermute x18, waiting for transfers between devices, extended_2(): lax.ppermute(head, axis, [((i + 1) % count, i) for i in range(ends)])  30.5 us
    dot_general x20, matrix products, block_product(): return jnp.einsum('nab,nbk->nak', matrices, field, precision=precise)  22.2 us
    dot_general x18, matrix products, coupled(): return jnp.einsum('nsab,nsbk->nak', coupling, picked, precision=precise)  16.8 us
    gather x18, local copies, waits for them, and re-layouts, coupled(): picked = jnp.take(extended, local_col, axis=0)  12.2 us
  transfers between devices with their start and end apart: 37, of which 33 were waited for; matrix products, arithmetic and copies ran while one was open for 1% of the time, Pallas kernels for 0%

commit v1 on v0

--- a/solution.py
+++ b/solution.py
@@ -59,7 +59,13 @@
         scatter_dimension=0,
         tiled=True,
     )
-    cross = lax.all_to_all(summed, "narrow", split_axis=0, concat_axis=2, tiled=True)
+    fit_plate_on_mesh = lambda device_axis, local_block: jnp.concatenate(
+        lax.all_to_all(
+            jnp.stack(jnp.split(local_block, lax.axis_size(device_axis), axis=0)), device_axis, 0, 0
+        ),
+        axis=2,
+    )
+    cross = fit_plate_on_mesh("narrow", summed)
     return (current.reshape(row_count, col_width), cross)
 
 

time: 330 us -> 331 us (level)
  no operation moved by 1% of the time
where the time goes in v1:
time: 331 us; the launch traced here: 329 us
  waiting for transfers between devices  124 us (37%)
  starting transfers between devices  118 us (36%)
  matrix products  40.1 us (12%)
  local copies, waits for them, and re-layouts  20 us (6%)
  between operations  17.1 us (5%)
  blocking collectives  6.33 us (2%)
    unnamed x2, waiting for transfers between devices  88.6 us
    ppermute x18, starting transfers between devices, extended_2(): lax.ppermute(head, axis, [((i + 1) % count, i) for i in range(ends)])  73.1 us
    ppermute x18, starting transfers between devices, extended_2(): lax.ppermute(tail, axis, [(i, (i + 1) % count) for i in range(ends)])  45.1 us
    ppermute x18, waiting for transfers between devices, extended_2(): lax.ppermute(head, axis, [((i + 1) % count, i) for i in range(ends)])  30.5 us
    dot_general x20, matrix products, block_product(): return jnp.einsum('nab,nbk->nak', matrices, field, precision=precise)  22.2 us
    dot_general x18, matrix products, coupled(): return jnp.einsum('nsab,nsbk->nak', coupling, picked, precision=precise)  16.9 us
    gather x18, local copies, waits for them, and re-layouts, coupled(): picked = jnp.take(extended, local_col, axis=0)  12.2 us
  transfers between devices with their start and end apart: 37, of which 33 were waited for; matrix products, arithmetic and copies ran while one was open for 1% of the time, Pallas kernels for 0%

profile of v1, /device:TPU:8, one launch (start us, length us, event | category | flops | bytes accessed | tf_op | source)
XLA Modules:
  0.0 328.9 jit_solution(14300190164345001334)
XLA Ops:
  7.2 1.4 fusion.107
  8.7 1.9 collective-permute-start
  10.6 4.5 %collective-permute-start.1 = (f32[192,128]{1,0:T(8,128)S(1)}, f32[192,128]{1,0:T(8,128)S(1)}, u32[]{:S(2)}, u32[]{:S(2)}) collective-permute-start(f32[192,128]{1,0:T(8,128)S(1)} %bitcast.397), channel_id=1, source_target_pairs={{2,0},{4,2},{6,4},{8,6},{10,8},{12,10},{14,12},{16,14},{18,16},{20... | collective-permute-start | bytes 294920 | tf_op jit(solution)/shard_map/ppermute | solution.py:20
  17.1 2.5 multiply_subtract_fusion
  23.3 1.9 collective-permute-start.2
  25.3 4.5 %collective-permute-start.3 = (f32[192,128]{1,0:T(8,128)S(1)}, f32[192,128]{1,0:T(8,128)S(1)}, u32[]{:S(2)}, u32[]{:S(2)}) collective-permute-start(f32[192,128]{1,0:T(8,128)S(1)} %bitcast.404), channel_id=1, source_target_pairs={{2,0},{4,2},{6,4},{8,6},{10,8},{12,10},{14,12},{16,14},{18,16},{20... | collective-permute-start | bytes 294920 | tf_op jit(solution)/shard_map/ppermute | solution.py:20
  30.2 1.8 collective-permute-done.3
  33.7 1.3 fusion.103
  35.0 1.9 collective-permute-start.4
  36.9 4.6 %collective-permute-start.5 = (f32[192,128]{1,0:T(8,128)S(1)}, f32[192,128]{1,0:T(8,128)S(1)}, u32[]{:S(2)}, u32[]{:S(2)}) collective-permute-start(f32[192,128]{1,0:T(8,128)S(1)} %bitcast.405), channel_id=1, source_target_pairs={{2,0},{4,2},{6,4},{8,6},{10,8},{12,10},{14,12},{16,14},{18,16},{20... | collective-permute-start | bytes 294920 | tf_op jit(solution)/shard_map/ppermute | solution.py:20
  41.9 1.8 collective-permute-done.5
  46.7 2.6 collective-permute-start.6
  49.4 3.9 %collective-permute-start.7 = (f32[192,128]{1,0:T(8,128)S(1)}, f32[192,128]{1,0:T(8,128)S(1)}, u32[]{:S(2)}, u32[]{:S(2)}) collective-permute-start(f32[192,128]{1,0:T(8,128)S(1)} %bitcast.406), channel_id=1, source_target_pairs={{2,0},{4,2},{6,4},{8,6},{10,8},{12,10},{14,12},{16,14},{18,16},{20... | collective-permute-start | bytes 294920 | tf_op jit(solution)/shard_map/ppermute | solution.py:20
  53.7 1.8 collective-permute-done.7
  58.5 2.6 collective-permute-start.8
  61.1 3.9 %collective-permute-start.9 = (f32[192,128]{1,0:T(8,128)S(1)}, f32[192,128]{1,0:T(8,128)S(1)}, u32[]{:S(2)}, u32[]{:S(2)}) collective-permute-start(f32[192,128]{1,0:T(8,128)S(1)} %bitcast.407), channel_id=1, source_target_pairs={{2,0},{4,2},{6,4},{8,6},{10,8},{12,10},{14,12},{16,14},{18,16},{20... | collective-permute-start | bytes 294920 | tf_op jit(solution)/shard_map/ppermute | solution.py:20
  65.4 1.8 collective-permute-done.9
  70.2 2.6 collective-permute-start.10
  72.8 3.9 %collective-permute-start.11 = (f32[192,128]{1,0:T(8,128)S(1)}, f32[192,128]{1,0:T(8,128)S(1)}, u32[]{:S(2)}, u32[]{:S(2)}) collective-permute-start(f32[192,128]{1,0:T(8,128)S(1)} %bitcast.408), channel_id=1, source_target_pairs={{2,0},{4,2},{6,4},{8,6},{10,8},{12,10},{14,12},{16,14},{18,16},{20... | collective-permute-start | bytes 294920 | tf_op jit(solution)/shard_map/ppermute | solution.py:20
  77.1 1.8 collective-permute-done.11
  80.7 1.3 fusion.95
  81.9 2.6 collective-permute-start.12
  84.6 3.9 %collective-permute-start.13 = (f32[192,128]{1,0:T(8,128)S(1)}, f32[192,128]{1,0:T(8,128)S(1)}, u32[]{:S(2)}, u32[]{:S(2)}) collective-permute-start(f32[192,128]{1,0:T(8,128)S(1)} %bitcast.409), channel_id=1, source_target_pairs={{2,0},{4,2},{6,4},{8,6},{10,8},{12,10},{14,12},{16,14},{18,16},{20... | collective-permute-start | bytes 294920 | tf_op jit(solution)/shard_map/ppermute | solution.py:20
  88.9 1.8 collective-permute-done.13
  92.4 1.3 fusion.93
  93.7 2.6 collective-permute-start.14
  96.3 4.1 %collective-permute-start.15 = (f32[192,128]{1,0:T(8,128)S(1)}, f32[192,128]{1,0:T(8,128)S(1)}, u32[]{:S(2)}, u32[]{:S(2)}) collective-permute-start(f32[192,128]{1,0:T(8,128)S(1)} %bitcast.410), channel_id=1, source_target_pairs={{2,0},{4,2},{6,4},{8,6},{10,8},{12,10},{14,12},{16,14},{18,16},{20... | collective-permute-start | bytes 294920 | tf_op jit(solution)/shard_map/ppermute | solution.py:20
  100.6 1.8 collective-permute-done.15
  104.1 1.3 fusion.91
  105.4 2.6 collective-permute-start.16
  108.0 3.9 %collective-permute-start.17 = (f32[192,128]{1,0:T(8,128)S(1)}, f32[192,128]{1,0:T(8,128)S(1)}, u32[]{:S(2)}, u32[]{:S(2)}) collective-permute-start(f32[192,128]{1,0:T(8,128)S(1)} %bitcast.402), channel_id=1, source_target_pairs={{2,0},{4,2},{6,4},{8,6},{10,8},{12,10},{14,12},{16,14},{18,16},{20... | collective-permute-start | bytes 294920 | tf_op jit(solution)/shard_map/ppermute | solution.py:20
  112.6 1.5 collective-permute-done.17
  117.8 2.6 collective-permute-start.18
  120.4 3.9 %collective-permute-start.19 = (f32[192,128]{1,0:T(8,128)S(1)}, f32[192,128]{1,0:T(8,128)S(1)}, u32[]{:S(2)}, u32[]{:S(2)}) collective-permute-start(f32[192,128]{1,0:T(8,128)S(1)} %bitcast.411), channel_id=1, source_target_pairs={{2,0},{4,2},{6,4},{8,6},{10,8},{12,10},{14,12},{16,14},{18,16},{20... | collective-permute-start | bytes 294920 | tf_op jit(solution)/shard_map/ppermute | solution.py:20
  124.7 1.8 collective-permute-done.19
  129.4 2.6 collective-permute-start.20
  132.0 3.9 %collective-permute-start.21 = (f32[192,128]{1,0:T(8,128)S(1)}, f32[192,128]{1,0:T(8,128)S(1)}, u32[]{:S(2)}, u32[]{:S(2)}) collective-permute-start(f32[192,128]{1,0:T(8,128)S(1)} %bitcast.412), channel_id=1, source_target_pairs={{2,0},{4,2},{6,4},{8,6},{10,8},{12,10},{14,12},{16,14},{18,16},{20... | collective-permute-start | bytes 294920 | tf_op jit(solution)/shard_map/ppermute | solution.py:20
  136.3 1.8 collective-permute-done.21
  139.9 1.3 fusion.85
  141.1 2.6 collective-permute-start.22
  143.8 3.9 %collective-permute-start.23 = (f32[192,128]{1,0:T(8,128)S(1)}, f32[192,128]{1,0:T(8,128)S(1)}, u32[]{:S(2)}, u32[]{:S(2)}) collective-permute-start(f32[192,128]{1,0:T(8,128)S(1)} %bitcast.413), channel_id=1, source_target_pairs={{2,0},{4,2},{6,4},{8,6},{10,8},{12,10},{14,12},{16,14},{18,16},{20... | collective-permute-start | bytes 294920 | tf_op jit(solution)/shard_map/ppermute | solution.py:20
  148.1 1.8 collective-permute-done.23
  151.6 1.3 fusion.83
  152.9 2.6 collective-permute-start.24
  155.5 3.9 %collective-permute-start.25 = (f32[192,128]{1,0:T(8,128)S(1)}, f32[192,128]{1,0:T(8,128)S(1)}, u32[]{:S(2)}, u32[]{:S(2)}) collective-permute-start(f32[192,128]{1,0:T(8,128)S(1)} %bitcast.414), channel_id=1, source_target_pairs={{2,0},{4,2},{6,4},{8,6},{10,8},{12,10},{14,12},{16,14},{18,16},{20... | collective-permute-start | bytes 294920 | tf_op jit(solution)/shard_map/ppermute | solution.py:20
  159.8 1.8 collective-permute-done.25
  163.3 1.3 fusion.81
  164.6 2.6 collective-permute-start.26
  167.2 3.9 %collective-permute-start.27 = (f32[192,128]{1,0:T(8,128)S(1)}, f32[192,128]{1,0:T(8,128)S(1)}, u32[]{:S(2)}, u32[]{:S(2)}) collective-permute-start(f32[192,128]{1,0:T(8,128)S(1)} %bitcast.415), channel_id=1, source_target_pairs={{2,0},{4,2},{6,4},{8,6},{10,8},{12,10},{14,12},{16,14},{18,16},{20... | collective-permute-start | bytes 294920 | tf_op jit(solution)/shard_map/ppermute | solution.py:20
  171.5 1.8 collective-permute-done.27
  176.4 2.6 collective-permute-start.28
  179.0 3.9 %collective-permute-start.29 = (f32[192,128]{1,0:T(8,128)S(1)}, f32[192,128]{1,0:T(8,128)S(1)}, u32[]{:S(2)}, u32[]{:S(2)}) collective-permute-start(f32[192,128]{1,0:T(8,128)S(1)} %bitcast.416), channel_id=1, source_target_pairs={{2,0},{4,2},{6,4},{8,6},{10,8},{12,10},{14,12},{16,14},{18,16},{20... | collective-permute-start | bytes 294920 | tf_op jit(solution)/shard_map/ppermute | solution.py:20
  183.3 1.8 collective-permute-done.29
  188.1 2.6 collective-permute-start.30
  190.7 4.2 %collective-permute-start.31 = (f32[192,128]{1,0:T(8,128)S(1)}, f32[192,128]{1,0:T(8,128)S(1)}, u32[]{:S(2)}, u32[]{:S(2)}) collective-permute-start(f32[192,128]{1,0:T(8,128)S(1)} %bitcast.417), channel_id=1, source_target_pairs={{2,0},{4,2},{6,4},{8,6},{10,8},{12,10},{14,12},{16,14},{18,16},{20... | collective-permute-start | bytes 294920 | tf_op jit(solution)/shard_map/ppermute | solution.py:20
  195.0 1.8 collective-permute-done.31
  199.8 2.6 collective-permute-start.32
  202.5 3.9 %collective-permute-start.33 = (f32[192,128]{1,0:T(8,128)S(1)}, f32[192,128]{1,0:T(8,128)S(1)}, u32[]{:S(2)}, u32[]{:S(2)}) collective-permute-start(f32[192,128]{1,0:T(8,128)S(1)} %bitcast.399), channel_id=1, source_target_pairs={{2,0},{4,2},{6,4},{8,6},{10,8},{12,10},{14,12},{16,14},{18,16},{20... | collective-permute-start | bytes 294920 | tf_op jit(solution)/shard_map/ppermute | solution.py:20
  207.2 1.4 collective-permute-done.33
  210.5 2.6 collective-permute-start.34
  213.2 3.9 %collective-permute-start.35 = (f32[192,128]{1,0:T(8,128)S(1)}, f32[192,128]{1,0:T(8,128)S(1)}, u32[]{:S(2)}, u32[]{:S(2)}) collective-permute-start(f32[192,128]{1,0:T(8,128)S(1)} %bitcast.400), channel_id=1, source_target_pairs={{2,0},{4,2},{6,4},{8,6},{10,8},{12,10},{14,12},{16,14},{18,16},{20... | collective-permute-start | bytes 294920 | tf_op jit(solution)/shard_map/ppermute | solution.py:20
  217.4 1.8 collective-permute-done.35
  225.7 88.6 %all-reduce.3.cloned.1.call-done = f32[64,2,128]{2,0,1:T(8,128)} async-done(((f32[64,2,128]{2,0,1:T(8,128)}), f32[64,2,128]{2,0,1:T(8,128)}) %all-reduce.3.cloned.1.call-update) | async-done | bytes 65552
  315.1 6.3 %all_to_all.5 = f32[2,2,2,128]{3,1,2,0:T(2,128)S(1)} all-to-all(f32[2,2,2,128]{3,1,2,0:T(2,128)S(1)} %pad_maximum_fusion.18), channel_id=1, replica_groups=mesh['blk'=16,'narrow'=2] {'narrow'}, dimensions={0} | all-to-all | bytes 8192 | tf_op jit(solution)/shard_map/all_to_all | solution.py:63
  (137 shorter events, 55.4 us)
Async XLA Ops:
  7.2 109.3 %copy-start = (f32[4,96,96]{2,1,0:T(8,128)S(1)}, f32[4,96,96]{2,1,0:T(8,128)}, u32[]{:S(2)}) copy-start(f32[4,96,96]{2,1,0:T(8,128)} %param.12) | copy-start | bytes 442372
  7.2 9.9 %copy-start.3 = (f32[4,3,96,96]{3,2,1,0:T(8,128)S(1)}, f32[4,3,96,96]{3,2,1,0:T(8,128)}, u32[]{:S(2)}) copy-start(f32[4,3,96,96]{3,2,1,0:T(8,128)} %param.14) | copy-start | bytes 1327108
  7.2 307.1 %all-reduce.3.cloned.1.call-start = ((), (), s32[]{:S(2)}) async-start(), calls=%async_computation.1 | async-start | bytes 131072
  8.7 10.9 %collective-permute-start = (f32[192,128]{1,0:T(8,128)S(1)}, f32[192,128]{1,0:T(8,128)S(1)}, u32[]{:S(2)}, u32[]{:S(2)}) collective-permute-start(f32[192,128]{1,0:T(8,128)S(1)} %bitcast.398), channel_id=1, source_target_pairs={{0,2},{2,4},{4,6},{6,8},{8,10},{10,12},{12,14},{14,16},{16,18},{18... | collective-permute-start | bytes 294920 | tf_op jit(solution)/shard_map/ppermute | solution.py:18
  10.6 9.0 %collective-permute-start.1 = (f32[192,128]{1,0:T(8,128)S(1)}, f32[192,128]{1,0:T(8,128)S(1)}, u32[]{:S(2)}, u32[]{:S(2)}) collective-permute-start(f32[192,128]{1,0:T(8,128)S(1)} %bitcast.397), channel_id=1, source_target_pairs={{2,0},{4,2},{6,4},{8,6},{10,8},{12,10},{14,12},{16,14},{18,16},{20... | collective-permute-start | bytes 294920 | tf_op jit(solution)/shard_map/ppermute | solution.py:20
  15.2 0.7 copy-start.7
  15.9 0.7 copy-start.8
  19.6 0.6 copy-start.4
  20.2 0.9 copy-start.2
  23.3 6.8 %collective-permute-start.2 = (f32[192,128]{1,0:T(8,128)S(1)}, f32[192,128]{1,0:T(8,128)S(1)}, u32[]{:S(2)}, u32[]{:S(2)}) collective-permute-start(f32[192,128]{1,0:T(8,128)S(1)} %bitcast.419), channel_id=1, source_target_pairs={{0,2},{2,4},{4,6},{6,8},{8,10},{10,12},{12,14},{14,16},{16,18},{18... | collective-permute-start | bytes 294920 | tf_op jit(solution)/shard_map/ppermute | solution.py:18
  25.3 6.7 %collective-permute-start.3 = (f32[192,128]{1,0:T(8,128)S(1)}, f32[192,128]{1,0:T(8,128)S(1)}, u32[]{:S(2)}, u32[]{:S(2)}) collective-permute-start(f32[192,128]{1,0:T(8,128)S(1)} %bitcast.404), channel_id=1, source_target_pairs={{2,0},{4,2},{6,4},{8,6},{10,8},{12,10},{14,12},{16,14},{18,16},{20... | collective-permute-start | bytes 294920 | tf_op jit(solution)/shard_map/ppermute | solution.py:20
  35.0 6.9 %collective-permute-start.4 = (f32[192,128]{1,0:T(8,128)S(1)}, f32[192,128]{1,0:T(8,128)S(1)}, u32[]{:S(2)}, u32[]{:S(2)}) collective-permute-start(f32[192,128]{1,0:T(8,128)S(1)} %bitcast.420), channel_id=1, source_target_pairs={{0,2},{2,4},{4,6},{6,8},{8,10},{10,12},{12,14},{14,16},{16,18},{18... | collective-permute-start | bytes 294920 | tf_op jit(solution)/shard_map/ppermute | solution.py:18
  36.9 6.8 %collective-permute-start.5 = (f32[192,128]{1,0:T(8,128)S(1)}, f32[192,128]{1,0:T(8,128)S(1)}, u32[]{:S(2)}, u32[]{:S(2)}) collective-permute-start(f32[192,128]{1,0:T(8,128)S(1)} %bitcast.405), channel_id=1, source_target_pairs={{2,0},{4,2},{6,4},{8,6},{10,8},{12,10},{14,12},{16,14},{18,16},{20... | collective-permute-start | bytes 294920 | tf_op jit(solution)/shard_map/ppermute | solution.py:20
  46.7 6.9 %collective-permute-start.6 = (f32[192,128]{1,0:T(8,128)S(1)}, f32[192,128]{1,0:T(8,128)S(1)}, u32[]{:S(2)}, u32[]{:S(2)}) collective-permute-start(f32[192,128]{1,0:T(8,128)S(1)} %bitcast.421), channel_id=1, source_target_pairs={{0,2},{2,4},{4,6},{6,8},{8,10},{10,12},{12,14},{14,16},{16,18},{18... | collective-permute-start | bytes 294920 | tf_op jit(solution)/shard_map/ppermute | solution.py:18
  49.4 6.1 %collective-permute-start.7 = (f32[192,128]{1,0:T(8,128)S(1)}, f32[192,128]{1,0:T(8,128)S(1)}, u32[]{:S(2)}, u32[]{:S(2)}) collective-permute-start(f32[192,128]{1,0:T(8,128)S(1)} %bitcast.406), channel_id=1, source_target_pairs={{2,0},{4,2},{6,4},{8,6},{10,8},{12,10},{14,12},{16,14},{18,16},{20... | collective-permute-start | bytes 294920 | tf_op jit(solution)/shard_map/ppermute | solution.py:20
  58.5 6.9 %collective-permute-start.8 = (f32[192,128]{1,0:T(8,128)S(1)}, f32[192,128]{1,0:T(8,128)S(1)}, u32[]{:S(2)}, u32[]{:S(2)}) collective-permute-start(f32[192,128]{1,0:T(8,128)S(1)} %bitcast.422), channel_id=1, source_target_pairs={{0,2},{2,4},{4,6},{6,8},{8,10},{10,12},{12,14},{14,16},{16,18},{18... | collective-permute-start | bytes 294920 | tf_op jit(solution)/shard_map/ppermute | solution.py:18
  61.1 6.1 %collective-permute-start.9 = (f32[192,128]{1,0:T(8,128)S(1)}, f32[192,128]{1,0:T(8,128)S(1)}, u32[]{:S(2)}, u32[]{:S(2)}) collective-permute-start(f32[192,128]{1,0:T(8,128)S(1)} %bitcast.407), channel_id=1, source_target_pairs={{2,0},{4,2},{6,4},{8,6},{10,8},{12,10},{14,12},{16,14},{18,16},{20... | collective-permute-start | bytes 294920 | tf_op jit(solution)/shard_map/ppermute | solution.py:20
  70.2 6.9 %collective-permute-start.10 = (f32[192,128]{1,0:T(8,128)S(1)}, f32[192,128]{1,0:T(8,128)S(1)}, u32[]{:S(2)}, u32[]{:S(2)}) collective-permute-start(f32[192,128]{1,0:T(8,128)S(1)} %bitcast.423), channel_id=1, source_target_pairs={{0,2},{2,4},{4,6},{6,8},{8,10},{10,12},{12,14},{14,16},{16,18},{18... | collective-permute-start | bytes 294920 | tf_op jit(solution)/shard_map/ppermute | solution.py:18
  72.8 6.1 %collective-permute-start.11 = (f32[192,128]{1,0:T(8,128)S(1)}, f32[192,128]{1,0:T(8,128)S(1)}, u32[]{:S(2)}, u32[]{:S(2)}) collective-permute-start(f32[192,128]{1,0:T(8,128)S(1)} %bitcast.408), channel_id=1, source_target_pairs={{2,0},{4,2},{6,4},{8,6},{10,8},{12,10},{14,12},{16,14},{18,16},{20... | collective-permute-start | bytes 294920 | tf_op jit(solution)/shard_map/ppermute | solution.py:20
  81.9 6.9 %collective-permute-start.12 = (f32[192,128]{1,0:T(8,128)S(1)}, f32[192,128]{1,0:T(8,128)S(1)}, u32[]{:S(2)}, u32[]{:S(2)}) collective-permute-start(f32[192,128]{1,0:T(8,128)S(1)} %bitcast.424), channel_id=1, source_target_pairs={{0,2},{2,4},{4,6},{6,8},{8,10},{10,12},{12,14},{14,16},{16,18},{18... | collective-permute-start | bytes 294920 | tf_op jit(solution)/shard_map/ppermute | solution.py:18
  84.6 6.1 %collective-permute-start.13 = (f32[192,128]{1,0:T(8,128)S(1)}, f32[192,128]{1,0:T(8,128)S(1)}, u32[]{:S(2)}, u32[]{:S(2)}) collective-permute-start(f32[192,128]{1,0:T(8,128)S(1)} %bitcast.409), channel_id=1, source_target_pairs={{2,0},{4,2},{6,4},{8,6},{10,8},{12,10},{14,12},{16,14},{18,16},{20... | collective-permute-start | bytes 294920 | tf_op jit(solution)/shard_map/ppermute | solution.py:20
  93.7 6.9 %collective-permute-start.14 = (f32[192,128]{1,0:T(8,128)S(1)}, f32[192,128]{1,0:T(8,128)S(1)}, u32[]{:S(2)}, u32[]{:S(2)}) collective-permute-start(f32[192,128]{1,0:T(8,128)S(1)} %bitcast.425), channel_id=1, source_target_pairs={{0,2},{2,4},{4,6},{6,8},{8,10},{10,12},{12,14},{14,16},{16,18},{18... | collective-permute-start | bytes 294920 | tf_op jit(solution)/shard_map/ppermute | solution.py:18
  96.3 6.1 %collective-permute-start.15 = (f32[192,128]{1,0:T(8,128)S(1)}, f32[192,128]{1,0:T(8,128)S(1)}, u32[]{:S(2)}, u32[]{:S(2)}) collective-permute-start(f32[192,128]{1,0:T(8,128)S(1)} %bitcast.410), channel_id=1, source_target_pairs={{2,0},{4,2},{6,4},{8,6},{10,8},{12,10},{14,12},{16,14},{18,16},{20... | collective-permute-start | bytes 294920 | tf_op jit(solution)/shard_map/ppermute | solution.py:20
  105.4 7.2 %collective-permute-start.16 = (f32[192,128]{1,0:T(8,128)S(1)}, f32[192,128]{1,0:T(8,128)S(1)}, u32[]{:S(2)}, u32[]{:S(2)}) collective-permute-start(f32[192,128]{1,0:T(8,128)S(1)} %bitcast.418), channel_id=1, source_target_pairs={{0,2},{2,4},{4,6},{6,8},{8,10},{10,12},{12,14},{14,16},{16,18},{18... | collective-permute-start | bytes 294920 | tf_op jit(solution)/shard_map/ppermute | solution.py:18
  108.0 6.1 %collective-permute-start.17 = (f32[192,128]{1,0:T(8,128)S(1)}, f32[192,128]{1,0:T(8,128)S(1)}, u32[]{:S(2)}, u32[]{:S(2)}) collective-permute-start(f32[192,128]{1,0:T(8,128)S(1)} %bitcast.402), channel_id=1, source_target_pairs={{2,0},{4,2},{6,4},{8,6},{10,8},{12,10},{14,12},{16,14},{18,16},{20... | collective-permute-start | bytes 294920 | tf_op jit(solution)/shard_map/ppermute | solution.py:20
  114.2 0.7 copy-start.5
  116.4 1.0 copy-start.1
  117.8 6.9 %collective-permute-start.18 = (f32[192,128]{1,0:T(8,128)S(1)}, f32[192,128]{1,0:T(8,128)S(1)}, u32[]{:S(2)}, u32[]{:S(2)}) collective-permute-start(f32[192,128]{1,0:T(8,128)S(1)} %bitcast.426), channel_id=1, source_target_pairs={{0,2},{2,4},{4,6},{6,8},{8,10},{10,12},{12,14},{14,16},{16,18},{18... | collective-permute-start | bytes 294920 | tf_op jit(solution)/shard_map/ppermute | solution.py:18
  120.4 6.1 %collective-permute-start.19 = (f32[192,128]{1,0:T(8,128)S(1)}, f32[192,128]{1,0:T(8,128)S(1)}, u32[]{:S(2)}, u32[]{:S(2)}) collective-permute-start(f32[192,128]{1,0:T(8,128)S(1)} %bitcast.411), channel_id=1, source_target_pairs={{2,0},{4,2},{6,4},{8,6},{10,8},{12,10},{14,12},{16,14},{18,16},{20... | collective-permute-start | bytes 294920 | tf_op jit(solution)/shard_map/ppermute | solution.py:20
  129.4 6.9 %collective-permute-start.20 = (f32[192,128]{1,0:T(8,128)S(1)}, f32[192,128]{1,0:T(8,128)S(1)}, u32[]{:S(2)}, u32[]{:S(2)}) collective-permute-start(f32[192,128]{1,0:T(8,128)S(1)} %bitcast.427), channel_id=1, source_target_pairs={{0,2},{2,4},{4,6},{6,8},{8,10},{10,12},{12,14},{14,16},{16,18},{18... | collective-permute-start | bytes 294920 | tf_op jit(solution)/shard_map/ppermute | solution.py:18
  132.0 6.1 %collective-permute-start.21 = (f32[192,128]{1,0:T(8,128)S(1)}, f32[192,128]{1,0:T(8,128)S(1)}, u32[]{:S(2)}, u32[]{:S(2)}) collective-permute-start(f32[192,128]{1,0:T(8,128)S(1)} %bitcast.412), channel_id=1, source_target_pairs={{2,0},{4,2},{6,4},{8,6},{10,8},{12,10},{14,12},{16,14},{18,16},{20... | collective-permute-start | bytes 294920 | tf_op jit(solution)/shard_map/ppermute | solution.py:20
  141.1 6.9 %collective-permute-start.22 = (f32[192,128]{1,0:T(8,128)S(1)}, f32[192,128]{1,0:T(8,128)S(1)}, u32[]{:S(2)}, u32[]{:S(2)}) collective-permute-start(f32[192,128]{1,0:T(8,128)S(1)} %bitcast.428), channel_id=1, source_target_pairs={{0,2},{2,4},{4,6},{6,8},{8,10},{10,12},{12,14},{14,16},{16,18},{18... | collective-permute-start | bytes 294920 | tf_op jit(solution)/shard_map/ppermute | solution.py:18
  143.8 6.1 %collective-permute-start.23 = (f32[192,128]{1,0:T(8,128)S(1)}, f32[192,128]{1,0:T(8,128)S(1)}, u32[]{:S(2)}, u32[]{:S(2)}) collective-permute-start(f32[192,128]{1,0:T(8,128)S(1)} %bitcast.413), channel_id=1, source_target_pairs={{2,0},{4,2},{6,4},{8,6},{10,8},{12,10},{14,12},{16,14},{18,16},{20... | collective-permute-start | bytes 294920 | tf_op jit(solution)/shard_map/ppermute | solution.py:20
  152.9 6.9 %collective-permute-start.24 = (f32[192,128]{1,0:T(8,128)S(1)}, f32[192,128]{1,0:T(8,128)S(1)}, u32[]{:S(2)}, u32[]{:S(2)}) collective-permute-start(f32[192,128]{1,0:T(8,128)S(1)} %bitcast.429), channel_id=1, source_target_pairs={{0,2},{2,4},{4,6},{6,8},{8,10},{10,12},{12,14},{14,16},{16,18},{18... | collective-permute-start | bytes 294920 | tf_op jit(solution)/shard_map/ppermute | solution.py:18
  155.5 6.1 %collective-permute-start.25 = (f32[192,128]{1,0:T(8,128)S(1)}, f32[192,128]{1,0:T(8,128)S(1)}, u32[]{:S(2)}, u32[]{:S(2)}) collective-permute-start(f32[192,128]{1,0:T(8,128)S(1)} %bitcast.414), channel_id=1, source_target_pairs={{2,0},{4,2},{6,4},{8,6},{10,8},{12,10},{14,12},{16,14},{18,16},{20... | collective-permute-start | bytes 294920 | tf_op jit(solution)/shard_map/ppermute | solution.py:20
  164.6 6.9 %collective-permute-start.26 = (f32[192,128]{1,0:T(8,128)S(1)}, f32[192,128]{1,0:T(8,128)S(1)}, u32[]{:S(2)}, u32[]{:S(2)}) collective-permute-start(f32[192,128]{1,0:T(8,128)S(1)} %bitcast.430), channel_id=1, source_target_pairs={{0,2},{2,4},{4,6},{6,8},{8,10},{10,12},{12,14},{14,16},{16,18},{18... | collective-permute-start | bytes 294920 | tf_op jit(solution)/shard_map/ppermute | solution.py:18
  167.2 6.1 %collective-permute-start.27 = (f32[192,128]{1,0:T(8,128)S(1)}, f32[192,128]{1,0:T(8,128)S(1)}, u32[]{:S(2)}, u32[]{:S(2)}) collective-permute-start(f32[192,128]{1,0:T(8,128)S(1)} %bitcast.415), channel_id=1, source_target_pairs={{2,0},{4,2},{6,4},{8,6},{10,8},{12,10},{14,12},{16,14},{18,16},{20... | collective-permute-start | bytes 294920 | tf_op jit(solution)/shard_map/ppermute | solution.py:20
  176.4 6.9 %collective-permute-start.28 = (f32[192,128]{1,0:T(8,128)S(1)}, f32[192,128]{1,0:T(8,128)S(1)}, u32[]{:S(2)}, u32[]{:S(2)}) collective-permute-start(f32[192,128]{1,0:T(8,128)S(1)} %bitcast.431), channel_id=1, source_target_pairs={{0,2},{2,4},{4,6},{6,8},{8,10},{10,12},{12,14},{14,16},{16,18},{18... | collective-permute-start | bytes 294920 | tf_op jit(solution)/shard_map/ppermute | solution.py:18
  179.0 6.1 %collective-permute-start.29 = (f32[192,128]{1,0:T(8,128)S(1)}, f32[192,128]{1,0:T(8,128)S(1)}, u32[]{:S(2)}, u32[]{:S(2)}) collective-permute-start(f32[192,128]{1,0:T(8,128)S(1)} %bitcast.416), channel_id=1, source_target_pairs={{2,0},{4,2},{6,4},{8,6},{10,8},{12,10},{14,12},{16,14},{18,16},{20... | collective-permute-start | bytes 294920 | tf_op jit(solution)/shard_map/ppermute | solution.py:20
  188.1 6.9 %collective-permute-start.30 = (f32[192,128]{1,0:T(8,128)S(1)}, f32[192,128]{1,0:T(8,128)S(1)}, u32[]{:S(2)}, u32[]{:S(2)}) collective-permute-start(f32[192,128]{1,0:T(8,128)S(1)} %bitcast.432), channel_id=1, source_target_pairs={{0,2},{2,4},{4,6},{6,8},{8,10},{10,12},{12,14},{14,16},{16,18},{18... | collective-permute-start | bytes 294920 | tf_op jit(solution)/shard_map/ppermute | solution.py:18
  190.7 6.1 %collective-permute-start.31 = (f32[192,128]{1,0:T(8,128)S(1)}, f32[192,128]{1,0:T(8,128)S(1)}, u32[]{:S(2)}, u32[]{:S(2)}) collective-permute-start(f32[192,128]{1,0:T(8,128)S(1)} %bitcast.417), channel_id=1, source_target_pairs={{2,0},{4,2},{6,4},{8,6},{10,8},{12,10},{14,12},{16,14},{18,16},{20... | collective-permute-start | bytes 294920 | tf_op jit(solution)/shard_map/ppermute | solution.py:20
  199.8 7.3 %collective-permute-start.32 = (f32[192,128]{1,0:T(8,128)S(1)}, f32[192,128]{1,0:T(8,128)S(1)}, u32[]{:S(2)}, u32[]{:S(2)}) collective-permute-start(f32[192,128]{1,0:T(8,128)S(1)} %bitcast.401), channel_id=1, source_target_pairs={{0,2},{2,4},{4,6},{6,8},{8,10},{10,12},{12,14},{14,16},{16,18},{18... | collective-permute-start | bytes 294920 | tf_op jit(solution)/shard_map/ppermute | solution.py:18
  202.5 6.1 %collective-permute-start.33 = (f32[192,128]{1,0:T(8,128)S(1)}, f32[192,128]{1,0:T(8,128)S(1)}, u32[]{:S(2)}, u32[]{:S(2)}) collective-permute-start(f32[192,128]{1,0:T(8,128)S(1)} %bitcast.399), channel_id=1, source_target_pairs={{2,0},{4,2},{6,4},{8,6},{10,8},{12,10},{14,12},{16,14},{18,16},{20... | collective-permute-start | bytes 294920 | tf_op jit(solution)/shard_map/ppermute | solution.py:20
  210.5 6.9 %collective-permute-start.34 = (f32[192,128]{1,0:T(8,128)S(1)}, f32[192,128]{1,0:T(8,128)S(1)}, u32[]{:S(2)}, u32[]{:S(2)}) collective-permute-start(f32[192,128]{1,0:T(8,128)S(1)} %bitcast.403), channel_id=1, source_target_pairs={{0,2},{2,4},{4,6},{6,8},{8,10},{10,12},{12,14},{14,16},{16,18},{18... | collective-permute-start | bytes 294920 | tf_op jit(solution)/shard_map/ppermute | solution.py:18
  213.2 6.1 %collective-permute-start.35 = (f32[192,128]{1,0:T(8,128)S(1)}, f32[192,128]{1,0:T(8,128)S(1)}, u32[]{:S(2)}, u32[]{:S(2)}) collective-permute-start(f32[192,128]{1,0:T(8,128)S(1)} %bitcast.400), channel_id=1, source_target_pairs={{2,0},{4,2},{6,4},{8,6},{10,8},{12,10},{14,12},{16,14},{18,16},{20... | collective-permute-start | bytes 294920 | tf_op jit(solution)/shard_map/ppermute | solution.py:20
  221.9 0.9 copy-start.6
  223.8 0.7 copy-start.9
Sparse Core Ops, SparseCore 0:
  223.9 90.2 all-reduce.2
